TPU v7x, 512 devices: a whole 4x8x8 slice. The times are simulated.
512 devices in a mesh: seq: 32 (over y, x), head: 16 (over z, core).
Axes of the slice: x: 4, y: 8, z: 8, core: 2. Of those that a mesh axis runs over, the one named last changes fastest.
Arguments:
- queries: bfloat16 [8192, 8192], P('seq', 'head'), may hold values from -1.796875 to 1.796875
- key_rows: bfloat16 [8192, 8192], P('seq', 'head'), may hold values from -1.796875 to 1.796875
- value_rows: bfloat16 [8192, 8192], P('seq', 'head'), may hold values from -6 to 6
- level_table: float32 [64, 7, 64], P(None, None, 'head'), may hold values from 0.25 to 4
- level_index: int32 [8192, 7], P('seq'), may hold values from 0 to 63
- norm_gain: float32 [8192], replicated, may hold values from 0.5 to 1.5
- cotangent: bfloat16 [8192, 8192], P(('seq', 'head')), may hold values from -6 to 6
Outputs:
- normed: bfloat16 [8192, 8192], P(('seq', 'head'))
- grad_query: bfloat16 [8192, 8192], P('seq', 'head')
- grad_key: bfloat16 [8192, 8192], P('seq', 'head')
- grad_value: bfloat16 [8192, 8192], P('seq', 'head')
- grad_table: float32 [64, 7, 64], P(None, None, 'head')
- grad_gain: float32 [8192], replicated
All inputs are finite; a program needn't handle non-finite values.
Results may differ from a plain program's by a relative error of at most 0.014.
Values may be sent and summed in bfloat16 or wider, within the bound.
A program may use at most 64 MiB of HBM per device.

v0:
```python
import jax
import jax.numpy as jnp
from jax import lax
from jax.sharding import PartitionSpec as P

CH = 128
LEVELS = 7
TABLE = 64
EPSILON = 1e-06
HIGHEST = lax.Precision.HIGHEST


def swapped(value, axis, bit):
    mask = 2**bit
    pairs = [(source, source ^ mask) for source in range(lax.axis_size(axis))]
    return lax.ppermute(value, axis, pairs)


def bit_length_of(values, places):
    result = jnp.zeros_like(values)
    for exponent in range(places):
        result = result + (values >= 1 << exponent).astype(jnp.int32)
    return result


def level_mask(spans):
    row_ids = lax.broadcasted_iota(jnp.int32, (spans, spans), 0)
    col_ids = lax.broadcasted_iota(jnp.int32, (spans, spans), 1)
    lengths = bit_length_of(jnp.bitwise_xor(row_ids, col_ids), 16)
    stacked = [((lengths == 1) & (col_ids < row_ids)).astype(jnp.float32)]
    return jnp.stack(stacked)


def body(queries, key_rows, value_rows, level_table, level_index, norm_gain, cotangent):
    tok_dev = queries.shape[0]
    head_count = level_table.shape[2]
    head_width = queries.shape[1] // head_count
    spans = tok_dev // CH
    local_bits = spans.bit_length() - 1
    seq_bits = lax.axis_size("seq").bit_length() - 1
    cross_count = LEVELS - 1 - local_bits
    shard_id = lax.axis_index("seq")
    query_blocks = queries.reshape(spans, CH, head_count, head_width)
    key_blocks = key_rows.reshape(spans, CH, head_count, head_width)
    value_blocks = value_rows.reshape(spans, CH, head_count, head_width)
    onehot = (level_index[:, :, None] == jnp.arange(TABLE, dtype=jnp.int32)[None, None, :]).astype(
        jnp.float32
    )
    weights = jnp.einsum("tlx,xlh->tlh", onehot, level_table, precision=HIGHEST)
    weights = weights.reshape(spans, CH, LEVELS, head_count)
    span_states = jnp.einsum(
        "icha,ichb->ihab", key_blocks, value_blocks, preferred_element_type=jnp.float32
    )
    masks_local = level_mask(spans)
    intra_states = jnp.einsum("mij,jhab->imhab", masks_local, span_states, precision=HIGHEST)
    shard_total = jnp.sum(span_states, axis=0)
    state_zeros = jnp.zeros((cross_count, head_count, head_width, head_width), jnp.float32)
    shards_in = lax.all_gather(
        shard_total[None].astype(jnp.bfloat16), "seq", axis=0, tiled=True
    ).astype(jnp.float32)
    source = jnp.arange(shards_in.shape[0], dtype=jnp.int32)
    lengths = bit_length_of(jnp.bitwise_xor(source, shard_id), 16)
    slot_of = jnp.minimum(lengths + local_bits, LEVELS - 1) - local_bits - 1
    selector = (slot_of[:, None] == jnp.arange(cross_count, dtype=jnp.int32)[None, :]) & (
        source < shard_id
    )[:, None]
    cross_states = state_zeros + jnp.einsum(
        "sk,shab->khab", selector.astype(jnp.float32), shards_in, precision=HIGHEST
    )
    spread = jnp.broadcast_to(cross_states[None], (spans,) + cross_states.shape)
    level_states = jnp.concatenate([intra_states, spread], axis=1).astype(jnp.bfloat16)
    far_out = jnp.einsum(
        "icha,ilhab->iclhb", query_blocks, level_states, preferred_element_type=jnp.float32
    )
    row_ids = lax.broadcasted_iota(jnp.int32, (CH, CH), 0)
    col_ids = lax.broadcasted_iota(jnp.int32, (CH, CH), 1)
    causal = col_ids <= row_ids
    scores = jnp.einsum(
        "icha,inha->ihcn", query_blocks, key_blocks, preferred_element_type=jnp.float32
    )
    scores = jnp.where(causal, scores, 0.0)
    near_out = jnp.einsum(
        "ihcn,inhb->ichb",
        scores.astype(jnp.bfloat16),
        value_blocks,
        preferred_element_type=jnp.float32,
    )
    level_out = jnp.concatenate([near_out[:, :, None], far_out], axis=2)
    attn = jnp.sum(weights[..., None] * level_out, axis=2).astype(jnp.bfloat16)
    attn_rows = attn.reshape(tok_dev, head_count * head_width)
    token_attn = lax.all_to_all(attn_rows, "head", split_axis=0, concat_axis=1, tiled=True)
    attn_f = token_attn.astype(jnp.float32)
    inv_rms = lax.rsqrt(jnp.mean(attn_f * attn_f, axis=1, keepdims=True) + EPSILON)
    unit_rows = attn_f * inv_rms
    normed = (unit_rows * norm_gain).astype(jnp.bfloat16)
    grad_out = cotangent.astype(jnp.float32)
    scaled = grad_out * norm_gain
    grad_gain = lax.psum(jnp.sum(grad_out * unit_rows, axis=0), ("seq", "head"))
    grad_attn = (
        (scaled - unit_rows * jnp.mean(scaled * unit_rows, axis=1, keepdims=True)) * inv_rms
    ).astype(jnp.bfloat16)
    head_grad = lax.all_to_all(grad_attn, "head", split_axis=1, concat_axis=0, tiled=True)
    grad_blocks = head_grad.reshape(spans, CH, head_count, head_width)
    grad_f = grad_blocks.astype(jnp.float32)
    grad_weight = jnp.sum(level_out * grad_f[:, :, None], axis=4)
    along_values = jnp.einsum(
        "ichb,inhb->ihcn", grad_blocks, value_blocks, preferred_element_type=jnp.float32
    )
    first_weight = jnp.transpose(weights[:, :, 0, :], (0, 2, 1))[..., None]
    grad_scores = jnp.where(causal, along_values * first_weight, 0.0).astype(jnp.bfloat16)
    weighted_scores = jnp.where(causal, scores * first_weight, 0.0).astype(jnp.bfloat16)
    near_dq = jnp.einsum(
        "ihcn,inha->icha", grad_scores, key_blocks, preferred_element_type=jnp.float32
    )
    near_dk = jnp.einsum(
        "ihcn,icha->inha", grad_scores, query_blocks, preferred_element_type=jnp.float32
    )
    near_dv = jnp.einsum(
        "ihcn,ichb->inhb", weighted_scores, grad_blocks, preferred_element_type=jnp.float32
    )
    far_dq = jnp.einsum(
        "ichb,ilhab->iclha", grad_blocks, level_states, preferred_element_type=jnp.float32
    )
    grad_query = near_dq + jnp.sum(weights[:, :, 1:, :, None] * far_dq, axis=2)
    scaled_grad = (weights[:, :, 1:, :, None] * grad_f[:, :, None]).astype(jnp.bfloat16)
    query_grads = jnp.einsum(
        "icha,iclhb->ilhab", query_blocks, scaled_grad, preferred_element_type=jnp.float32
    )
    inner_grad = jnp.einsum(
        "mij,imhab->jhab", masks_local, query_grads[:, :local_bits], precision=HIGHEST
    )
    shard_grads = jnp.sum(query_grads[:, local_bits:], axis=0)
    cross_grad = jnp.zeros((head_count, head_width, head_width), jnp.float32)
    group_grads = shard_grads
    for bit_pos in range(seq_bits):
        partner = swapped(group_grads.astype(jnp.bfloat16), "seq", bit_pos).astype(
            group_grads.dtype
        )
        lower_half = 1.0 - jnp.bitwise_and(jnp.right_shift(shard_id, bit_pos), 1).astype(
            jnp.float32
        )
        level_slot = min(bit_pos, cross_count - 1)
        cross_grad = cross_grad + lower_half * partner[level_slot]
        group_grads = group_grads + partner
    key_state = (inner_grad + cross_grad[None]).astype(jnp.bfloat16)
    grad_key = near_dk + jnp.einsum(
        "jhab,jnhb->jnha", key_state, value_blocks, preferred_element_type=jnp.float32
    )
    grad_value = near_dv + jnp.einsum(
        "jhab,jnha->jnhb", key_state, key_blocks, preferred_element_type=jnp.float32
    )
    table_part = jnp.einsum(
        "tlx,tlh->xlh", onehot, grad_weight.reshape(tok_dev, LEVELS, head_count), precision=HIGHEST
    )
    grad_table = lax.psum(table_part, "seq")
    row_shape = (tok_dev, head_count * head_width)
    return (
        normed,
        grad_query.astype(jnp.bfloat16).reshape(row_shape),
        grad_key.astype(jnp.bfloat16).reshape(row_shape),
        grad_value.astype(jnp.bfloat16).reshape(row_shape),
        grad_table,
        grad_gain,
    )


def solution(mesh):
    placed = (
        P("seq", "head"),
        P("seq", "head"),
        P("seq", "head"),
        P(None, None, "head"),
        P("seq", None),
        P(),
        P(("seq", "head"), None),
    )
    return jax.shard_map(
        body,
        mesh=mesh,
        in_specs=placed,
        out_specs=(
            P(("seq", "head"), None),
            P("seq", "head"),
            P("seq", "head"),
            P("seq", "head"),
            P(None, None, "head"),
            P(),
        ),
        check_vma=False,
    )
```

profile of v0, /device:TPU:32, one launch (start us, length us, event | category | flops | bytes accessed | tf_op | source)
XLA Modules:
  0.0 519.8 jit_solution(9532326248119924726)
XLA Ops:
  7.2 1.1 reshape.150
  10.7 1.3 fusion.16
  13.8 86.5 %all-gather.3.cloned.1.call-done = bf16[128,128,128]{2,1,0:T(8,128)(2,1)} async-done(((bf16[4,128,128]{2,1,0:T(8,128)(2,1)}), bf16[128,128,128]{2,1,0:T(8,128)(2,1)}) %all-gather.3.cloned.1.call-update) | async-done | bytes 4194320 | tf_op jit(solution)/shard_map/all_gather | solution.py:58
  100.3 4.5 fusion.5
  107.4 1.7 copy-done.1
  110.0 18.5 %all_to_all.26 = bf16[16,16,512]{2,1,0:T(8,128)(2,1)S(1)} all-to-all(bf16[16,16,512]{2,1,0:T(8,128)(2,1)S(1)} %convert_element_type.402), channel_id=1, replica_groups=mesh['seq'=32,'head'=16] {'head'}, dimensions={0} | all-to-all | bytes 524288 | tf_op jit(solution)/shard_map/all_to_all | solution.py:91
  130.7 3.5 all-to-all-start.1
  134.3 11.3 %all-to-all-done.1 = bf16[16,16,512]{2,0,1:T(8,128)(2,1)S(1)} async-done(((bf16[16,16,512]{2,0,1:T(8,128)(2,1)}), bf16[16,16,512]{2,0,1:T(8,128)(2,1)S(1)}, u32[]{:S(2)}, u32[]{:S(2)}) %all-to-all-start.1) | async-done | bytes 262176 | tf_op jit(solution)/shard_map/all_to_all | solution.py:102
  147.7 1.4 copy-done.3
  149.2 2.8 collective-permute-start
  152.0 16.3 %collective-permute-done = bf16[5,4,128,128]{2,3,0,1:T(8,128)(2,1)S(1)} collective-permute-done((bf16[5,4,128,128]{2,3,0,1:T(8,128)(2,1)S(1)}, bf16[5,4,128,128]{2,3,0,1:T(8,128)(2,1)S(1)}, u32[]{:S(2)}, u32[]{:S(2)}) %collective-permute-start) | collective-permute-done | bytes 655392 | tf_op jit(solution)/shard_map/ppermute | solution.py:16
  169.4 4.0 collective-permute-start.1
  173.4 16.0 %collective-permute-done.1 = bf16[5,4,128,128]{2,3,0,1:T(8,128)(2,1)S(1)} collective-permute-done((bf16[5,4,128,128]{2,3,0,1:T(8,128)(2,1)}, bf16[5,4,128,128]{2,3,0,1:T(8,128)(2,1)S(1)}, u32[]{:S(2)}, u32[]{:S(2)}) %collective-permute-start.1) | collective-permute-done | bytes 655392 | tf_op jit(solution)/shard_map/ppermute | solution.py:16
  189.4 1.1 fusion.27
  190.5 4.0 collective-permute-start.2
  194.5 100.7 %psum.15 = f32[8192]{0:T(1024)} all-reduce(f32[8192]{0:T(1024)S(1)} %get-tuple-element.6), channel_id=1, replica_groups=mesh['seq'=32,'head'=16] {'seq','head'}, use_global_device_ids=true, to_apply=%region_9.10 | all-reduce | flops 8192 | bytes 65536 | tf_op jit(solution)/shard_map/psum | solution.py:98
  295.2 3.0 fusion.2
  298.2 2.0 copy.219
  300.3 1.3 fusion.11
  301.6 2.5 fusion.26
  304.0 2.5 collective-permute-start.3
  308.4 1.9 slice_bitcast_fusion
  310.3 2.0 copy.226
  312.3 25.5 %collective-permute-done.3 = bf16[5,4,128,128]{2,3,0,1:T(8,128)(2,1)} collective-permute-done((bf16[5,4,128,128]{2,3,0,1:T(8,128)(2,1)}, bf16[5,4,128,128]{2,3,0,1:T(8,128)(2,1)}, u32[]{:S(2)}, u32[]{:S(2)}) %collective-permute-start.3) | collective-permute-done | bytes 655392 | tf_op jit(solution)/shard_map/ppermute | solution.py:16
  337.8 2.6 add_convert_fusion
  340.4 4.2 collective-permute-start.4
  344.9 157.1 %psum.14 = f32[64,7,4]{0,2,1:T(4,128)} all-reduce(f32[64,7,4]{0,2,1:T(4,128)S(1)} %convolution_bitcast_fusion.7), channel_id=1, replica_groups=mesh['seq'=32,'head'=16] {'seq'}, use_global_device_ids=true, to_apply=%region_7.8 | all-reduce | flops 1792 | bytes 14336 | tf_op jit(solution)/shard_map/psum | solution.py:155
  502.0 2.1 fusion.61
  504.1 2.4 fusion.28
  506.8 1.2 convert_element_type.422
  508.0 1.2 convert_element_type.425
  509.2 1.1 fusion.31
  (95 shorter events, 17.8 us)
Async XLA Ops:
  7.2 3.1 copy-start
  7.2 3.1 copy-start.19
  7.2 3.4 copy-start.17
  7.2 93.1 %all-gather.3.cloned.1.call-start = ((), (), s32[]{:S(2)}) async-start(), calls=%async_computation.2 | async-start | bytes 4325376 | tf_op jit(solution)/shard_map/all_gather | solution.py:58
  12.2 93.5 %copy-start.15 = (bf16[2,1,4,128,128]{3,4,1,2,0:T(8,128)(2,1)}, bf16[2,1,4,128,128]{3,4,1,2,0:T(8,128)(2,1)S(1)}, u32[]{:S(2)}) copy-start(bf16[2,1,4,128,128]{3,4,1,2,0:T(8,128)(2,1)S(1)} %copy.206) | copy-start | bytes 786436
  12.6 0.8 copy-start.5
  13.8 93.6 %copy-start.6 = (f32[2,128,1,4,128]{1,4,2,3,0:T(8,128)}, f32[2,128,1,4,128]{1,4,2,3,0:T(8,128)S(1)}, u32[]{:S(2)}) copy-start(f32[2,128,1,4,128]{1,4,2,3,0:T(8,128)S(1)} %convolution_bitcast_fusion.5) | copy-start | bytes 1572868
  105.8 1.0 copy-start.4
  107.4 1.7 copy-start.1
  109.8 18.9 %copy-start.16 = (bf16[16,8192]{1,0:T(8,128)(2,1)S(1)}, bf16[16,8192]{1,0:T(8,128)(2,1)}, u32[]{:S(2)}) copy-start(bf16[16,8192]{1,0:T(8,128)(2,1)} %param.13) | copy-start | bytes 786436
  109.9 18.9 %copy-start.18 = (f32[8192]{0:T(1024)S(1)}, f32[8192]{0:T(1024)}, u32[]{:S(2)}) copy-start(f32[8192]{0:T(1024)} %param.12) | copy-start | bytes 98308
  130.7 14.9 %all-to-all-start.1 = ((bf16[16,16,512]{2,0,1:T(8,128)(2,1)}), bf16[16,16,512]{2,0,1:T(8,128)(2,1)S(1)}, u32[]{:S(2)}, u32[]{:S(2)}) async-start(bf16[16,16,512]{2,0,1:T(8,128)(2,1)} %bitcast.93), calls=%async_computation.1 | async-start | bytes 524288 | tf_op jit(solution)/shard_map/all_to_all | solution.py:102
  145.7 0.7 copy-start.10
  146.6 0.8 copy-start.8
  147.5 1.6 copy-start.3
  149.2 19.2 %collective-permute-start = (bf16[5,4,128,128]{2,3,0,1:T(8,128)(2,1)S(1)}, bf16[5,4,128,128]{2,3,0,1:T(8,128)(2,1)S(1)}, u32[]{:S(2)}, u32[]{:S(2)}) collective-permute-start(bf16[5,4,128,128]{2,3,0,1:T(8,128)(2,1)S(1)} %convert_element_type.415), channel_id=1, source_target_pairs={{0,16},{16,0},{32,48},{48,32},{64,80},{80,64},{96,112},{112,96},{1... | collective-permute-start | bytes 1966088 | tf_op jit(solution)/shard_map/ppermute | solution.py:16
  169.4 20.0 %collective-permute-start.1 = (bf16[5,4,128,128]{2,3,0,1:T(8,128)(2,1)}, bf16[5,4,128,128]{2,3,0,1:T(8,128)(2,1)S(1)}, u32[]{:S(2)}, u32[]{:S(2)}) collective-permute-start(bf16[5,4,128,128]{2,3,0,1:T(8,128)(2,1)} %fusion.56), channel_id=1, source_target_pairs={{0,32},{16,48},{32,0},{48,16},{64,96},{80,112},{96,64},{112,80},{1... | collective-permute-start | bytes 1966088 | tf_op jit(solution)/shard_map/ppermute | solution.py:16
  190.5 111.1 %collective-permute-start.2 = (bf16[5,4,128,128]{2,3,0,1:T(8,128)(2,1)}, bf16[5,4,128,128]{2,3,0,1:T(8,128)(2,1)}, u32[]{:S(2)}, u32[]{:S(2)}) collective-permute-start(bf16[5,4,128,128]{2,3,0,1:T(8,128)(2,1)} %fusion.27), channel_id=1, source_target_pairs={{0,64},{16,80},{32,96},{48,112},{64,0},{80,16},{96,32},{112,48},{1... | collective-permute-start | bytes 1966088 | tf_op jit(solution)/shard_map/ppermute | solution.py:16
  301.5 5.0 copy-start.13
  301.6 5.0 copy-start.12
  301.6 6.1 %copy-start.2 = (f32[2,128,6,4,128]{1,4,2,3,0:T(8,128)S(1)}, f32[2,128,6,4,128]{1,4,2,3,0:T(8,128)}, u32[]{:S(2)}) copy-start(f32[2,128,6,4,128]{1,4,2,3,0:T(8,128)} %copy-done.1) | copy-start | bytes 9437188
  304.0 3.7 copy-start.7
  304.0 3.7 copy-start.9
  304.0 33.8 %collective-permute-start.3 = (bf16[5,4,128,128]{2,3,0,1:T(8,128)(2,1)}, bf16[5,4,128,128]{2,3,0,1:T(8,128)(2,1)}, u32[]{:S(2)}, u32[]{:S(2)}) collective-permute-start(bf16[5,4,128,128]{2,3,0,1:T(8,128)(2,1)} %fusion.26), channel_id=1, source_target_pairs={{0,128},{16,144},{32,160},{48,176},{64,192},{80,208},{96,224},{112... | collective-permute-start | bytes 1966088 | tf_op jit(solution)/shard_map/ppermute | solution.py:16
  340.4 168.8 %collective-permute-start.4 = (bf16[5,4,128,128]{2,3,0,1:T(8,128)(2,1)}, bf16[5,4,128,128]{2,3,0,1:T(8,128)(2,1)}, u32[]{:S(2)}, u32[]{:S(2)}) collective-permute-start(bf16[5,4,128,128]{2,3,0,1:T(8,128)(2,1)} %add_convert_fusion), channel_id=1, source_target_pairs={{0,256},{16,272},{32,288},{48,304},{64,320},{80,336},{96,352},{112... | collective-permute-start | bytes 1966088 | tf_op jit(solution)/shard_map/ppermute | solution.py:16
  509.2 1.5 copy-start.11
  510.4 1.0 copy-start.14
Sparse Core Ops, SparseCore 0:
  11.8 88.4 all-gather.2
where the time goes:
time: 521 us; the launch traced here: 520 us
  blocking collectives  276 us (53%)
  waiting for transfers between devices  156 us (30%)
  starting transfers between devices  21.1 us (4%)
  local copies, waits for them, and re-layouts  19.3 us (4%)
  matrix products  19 us (4%)
  between operations  14.6 us (3%)
  other arithmetic  13.9 us (3%)
    psum x1, blocking collectives, body(): grad_table = lax.psum(table_part, 'seq')  157 us
    psum x1, blocking collectives, body(): grad_gain = lax.psum(jnp.sum(grad_out * unit_rows, axis=0), ('seq', 'head'))  101 us
    all_gather x1, waiting for transfers between devices, body(): lax.all_gather(shard_total[None].astype(jnp.bfloat16), 'seq', axis=0, til...  86.5 us
    ppermute x5, waiting for transfers between devices, swapped(): return lax.ppermute(value, axis, pairs)  57.8 us
    all_to_all x1, blocking collectives, body(): lax.all_to_all(attn_rows, 'head', split_axis=0, concat_axis=1, tiled=True)  18.5 us
    ppermute x5, starting transfers between devices, swapped(): return lax.ppermute(value, axis, pairs)  17.5 us
    all_to_all x1, waiting for transfers between devices, body(): lax.all_to_all(grad_attn, 'head', split_axis=1, concat_axis=0, tiled=True)  11.3 us
  transfers between devices with their start and end apart: 7, of which 5 were waited for; matrix products, arithmetic and copies ran while one was open for 4% of the time, Pallas kernels for 0%

commit v1 on v0

--- a/solution.py
+++ b/solution.py
@@ -152,7 +152,10 @@
     table_part = jnp.einsum(
         "tlx,tlh->xlh", onehot, grad_weight.reshape(tok_dev, LEVELS, head_count), precision=HIGHEST
     )
-    grad_table = lax.psum(table_part, "seq")
+    peers, grad_table = (lax.axis_size("seq"), table_part)
+    for far in [1 << k for k in range(peers.bit_length() - 1)]:
+        pairs_2 = [(i, i ^ far) for i in range(peers)]
+        grad_table = grad_table + lax.ppermute(grad_table, "seq", pairs_2)
     row_shape = (tok_dev, head_count * head_width)
     return (
         normed,

time: 521 us -> 402 us (0.77)
  the two profiles are of different devices: /device:TPU:32 before, /device:TPU:1 now
where the time goes in v1:
time: 402 us; the launch traced here: 401 us
  waiting for transfers between devices  177 us (44%)
  blocking collectives  123 us (31%)
  starting transfers between devices  37.7 us (9%)
  local copies, waits for them, and re-layouts  16.7 us (4%)
  other arithmetic  16.6 us (4%)
  matrix products  15.2 us (4%)
  between operations  14.7 us (4%)
    psum x1, blocking collectives, body(): grad_gain = lax.psum(jnp.sum(grad_out * unit_rows, axis=0), ('seq', 'head'))  101 us
    all_gather x1, waiting for transfers between devices, body(): lax.all_gather(shard_total[None].astype(jnp.bfloat16), 'seq', axis=0, til...  87.9 us
    ppermute x5, waiting for transfers between devices, swapped(): return lax.ppermute(value, axis, pairs)  48.2 us
    ppermute x5, waiting for transfers between devices, body(): grad_table = grad_table + lax.ppermute(grad_table, 'seq', pairs_2)  29.6 us
    all_to_all x1, blocking collectives, body(): lax.all_to_all(attn_rows, 'head', split_axis=0, concat_axis=1, tiled=True)  22.1 us
    ppermute x5, starting transfers between devices, body(): grad_table = grad_table + lax.ppermute(grad_table, 'seq', pairs_2)  17.9 us
    ppermute x5, starting transfers between devices, swapped(): return lax.ppermute(value, axis, pairs)  16.3 us
    all_to_all x1, waiting for transfers between devices, body(): lax.all_to_all(grad_attn, 'head', split_axis=1, concat_axis=0, tiled=True)  11.1 us
  transfers between devices with their start and end apart: 12, of which 7 were waited for; matrix products, arithmetic and copies ran while one was open for 6% of the time, Pallas kernels for 0%

profile of v1, /device:TPU:1, one launch (start us, length us, event | category | flops | bytes accessed | tf_op | source)
XLA Modules:
  0.0 401.0 jit_solution(689504358488497827)
XLA Ops:
  10.7 1.3 fusion.16
  13.8 87.9 %all-gather.3.cloned.1.call-done = bf16[128,128,128]{2,1,0:T(8,128)(2,1)} async-done(((bf16[4,128,128]{2,1,0:T(8,128)(2,1)}), bf16[128,128,128]{2,1,0:T(8,128)(2,1)}) %all-gather.3.cloned.1.call-update) | async-done | bytes 4194320 | tf_op jit(solution)/shard_map/all_gather | solution.py:58
  101.7 4.5 %fusion.5 = bf16[5,4,128,128]{3,0,2,1:T(8,128)(2,1)S(1)} fusion(bf16[32,4,128,128]{3,2,1,0:T(8,128)(2,1)} %bitcast.98, s32[32]{0:T(128)S(1)} %fusion.97, pred[32]{0:T(512)(128)(4,1)S(1)} %iota_compare_fusion.5), kind=kOutput, calls=%fused_computation.14 | convolution fusion | flops 21299520 | bytes 4849824 | tf_op jit(solution)/shard_map/sk,shab->khab/dot_general | solution.py:67
  108.9 1.7 copy-done.1
  111.4 22.1 %all_to_all.26 = bf16[16,16,512]{2,1,0:T(8,128)(2,1)S(1)} all-to-all(bf16[16,16,512]{2,1,0:T(8,128)(2,1)S(1)} %convert_element_type.402), channel_id=1, replica_groups=mesh['seq'=32,'head'=16] {'head'}, dimensions={0} | all-to-all | bytes 524288 | tf_op jit(solution)/shard_map/all_to_all | solution.py:91
  135.8 3.4 all-to-all-start.1
  139.3 11.1 %all-to-all-done.1 = bf16[16,16,512]{2,0,1:T(8,128)(2,1)S(1)} async-done(((bf16[16,16,512]{2,0,1:T(8,128)(2,1)}), bf16[16,16,512]{2,0,1:T(8,128)(2,1)S(1)}, u32[]{:S(2)}, u32[]{:S(2)}) %all-to-all-start.1) | async-done | bytes 262176 | tf_op jit(solution)/shard_map/all_to_all | solution.py:102
  152.4 1.4 copy-done.2
  153.9 1.9 collective-permute-start
  155.9 16.4 %collective-permute-done = bf16[5,4,128,128]{2,3,0,1:T(8,128)(2,1)S(1)} collective-permute-done((bf16[5,4,128,128]{2,3,0,1:T(8,128)(2,1)S(1)}, bf16[5,4,128,128]{2,3,0,1:T(8,128)(2,1)S(1)}, u32[]{:S(2)}, u32[]{:S(2)}) %collective-permute-start) | collective-permute-done | bytes 655392 | tf_op jit(solution)/shard_map/ppermute | solution.py:16
  173.3 3.1 collective-permute-start.1
  176.4 16.0 %collective-permute-done.1 = bf16[5,4,128,128]{2,3,0,1:T(8,128)(2,1)S(1)} collective-permute-done((bf16[5,4,128,128]{2,3,0,1:T(8,128)(2,1)}, bf16[5,4,128,128]{2,3,0,1:T(8,128)(2,1)S(1)}, u32[]{:S(2)}, u32[]{:S(2)}) %collective-permute-start.1) | collective-permute-done | bytes 655392 | tf_op jit(solution)/shard_map/ppermute | solution.py:16
  193.6 3.5 collective-permute-start.2
  197.1 101.3 %psum.7 = f32[8192]{0:T(1024)} all-reduce(f32[8192]{0:T(1024)S(1)} %get-tuple-element.6), channel_id=1, replica_groups=mesh['seq'=32,'head'=16] {'seq','head'}, use_global_device_ids=true, to_apply=%region_8.9 | all-reduce | flops 8192 | bytes 65536 | tf_op jit(solution)/shard_map/psum | solution.py:98
  298.3 2.7 multiply_reduce_fusion
  301.4 2.8 collective-permute-start.5
  304.2 2.3 fusion.26
  306.5 2.5 collective-permute-start.3
  309.0 1.2 fusion.28
  311.2 3.1 collective-permute-start.6
  314.4 1.6 fusion.2
  316.0 2.0 copy.219
  318.0 5.4 %collective-permute-start.7 = (f32[64,7,4]{0,2,1:T(4,128)S(1)}, f32[64,7,4]{0,2,1:T(4,128)S(1)}, u32[]{:S(2)}, u32[]{:S(2)}) collective-permute-start(f32[64,7,4]{0,2,1:T(4,128)S(1)} %add.361), channel_id=1, source_target_pairs={{0,64},{16,80},{32,96},{48,112},{64,0},{80,16},{96,32},{112,48},{1... | collective-permute-start | bytes 21512 | tf_op jit(solution)/shard_map/ppermute | solution.py:158
  323.4 15.8 %collective-permute-done.3 = bf16[5,4,128,128]{2,3,0,1:T(8,128)(2,1)} collective-permute-done((bf16[5,4,128,128]{2,3,0,1:T(8,128)(2,1)}, bf16[5,4,128,128]{2,3,0,1:T(8,128)(2,1)}, u32[]{:S(2)}, u32[]{:S(2)}) %collective-permute-start.3) | collective-permute-done | bytes 655392 | tf_op jit(solution)/shard_map/ppermute | solution.py:16
  339.2 2.6 add_convert_fusion
  341.8 5.4 %collective-permute-start.4 = (bf16[5,4,128,128]{2,3,0,1:T(8,128)(2,1)}, bf16[5,4,128,128]{2,3,0,1:T(8,128)(2,1)}, u32[]{:S(2)}, u32[]{:S(2)}) collective-permute-start(bf16[5,4,128,128]{2,3,0,1:T(8,128)(2,1)} %add_convert_fusion), channel_id=1, source_target_pairs={{0,256},{16,272},{32,288},{48,304},{64,320},{80,336},{96,352},{112... | collective-permute-start | bytes 1966088 | tf_op jit(solution)/shard_map/ppermute | solution.py:16
  347.5 1.9 collective-permute-start.8
  350.7 28.0 %collective-permute-done.8 = f32[64,7,4]{0,2,1:T(4,128)S(1)} collective-permute-done((f32[64,7,4]{0,2,1:T(4,128)S(1)}, f32[64,7,4]{0,2,1:T(4,128)S(1)}, u32[]{:S(2)}, u32[]{:S(2)}) %collective-permute-start.8) | collective-permute-done | bytes 7200 | tf_op jit(solution)/shard_map/ppermute | solution.py:158
  378.7 4.7 %collective-permute-start.9 = (f32[64,7,4]{0,2,1:T(4,128)S(1)}, f32[64,7,4]{0,2,1:T(4,128)S(1)}, u32[]{:S(2)}, u32[]{:S(2)}) collective-permute-start(f32[64,7,4]{0,2,1:T(4,128)S(1)} %add.363), channel_id=1, source_target_pairs={{0,256},{16,272},{32,288},{48,304},{64,320},{80,336},{96,352},{112... | collective-permute-start | bytes 21512 | tf_op jit(solution)/shard_map/ppermute | solution.py:158
  385.5 1.6 collective-permute-done.9
  388.0 1.2 convert_element_type.422
  389.2 1.2 convert_element_type.425
  (111 shorter events, 24.7 us)
Async XLA Ops:
  7.2 3.1 copy-start
  7.2 3.1 copy-start.20
  7.2 3.4 copy-start.18
  7.2 94.5 %all-gather.3.cloned.1.call-start = ((), (), s32[]{:S(2)}) async-start(), calls=%async_computation.2 | async-start | bytes 4325376 | tf_op jit(solution)/shard_map/all_gather | solution.py:58
  12.2 95.0 %copy-start.15 = (bf16[2,1,4,128,128]{3,4,1,2,0:T(8,128)(2,1)}, bf16[2,1,4,128,128]{3,4,1,2,0:T(8,128)(2,1)S(1)}, u32[]{:S(2)}) copy-start(bf16[2,1,4,128,128]{3,4,1,2,0:T(8,128)(2,1)S(1)} %copy.206) | copy-start | bytes 786436
  12.6 0.8 copy-start.5
  13.8 95.1 %copy-start.7 = (f32[2,128,1,4,128]{1,4,2,3,0:T(8,128)}, f32[2,128,1,4,128]{1,4,2,3,0:T(8,128)S(1)}, u32[]{:S(2)}) copy-start(f32[2,128,1,4,128]{1,4,2,3,0:T(8,128)S(1)} %convolution_bitcast_fusion.5) | copy-start | bytes 1572868
  107.2 1.1 copy-start.3
  108.9 1.7 copy-start.1
  111.3 22.5 %copy-start.17 = (bf16[16,8192]{1,0:T(8,128)(2,1)S(1)}, bf16[16,8192]{1,0:T(8,128)(2,1)}, u32[]{:S(2)}) copy-start(bf16[16,8192]{1,0:T(8,128)(2,1)} %param.13) | copy-start | bytes 786436
  111.3 22.5 %copy-start.19 = (f32[8192]{0:T(1024)S(1)}, f32[8192]{0:T(1024)}, u32[]{:S(2)}) copy-start(f32[8192]{0:T(1024)} %param.12) | copy-start | bytes 98308
  135.8 14.6 %all-to-all-start.1 = ((bf16[16,16,512]{2,0,1:T(8,128)(2,1)}), bf16[16,16,512]{2,0,1:T(8,128)(2,1)S(1)}, u32[]{:S(2)}, u32[]{:S(2)}) async-start(bf16[16,16,512]{2,0,1:T(8,128)(2,1)} %bitcast.93), calls=%async_computation.1 | async-start | bytes 524288 | tf_op jit(solution)/shard_map/all_to_all | solution.py:102
  151.4 0.8 copy-start.8
  152.2 1.6 copy-start.2
  153.9 18.3 %collective-permute-start = (bf16[5,4,128,128]{2,3,0,1:T(8,128)(2,1)S(1)}, bf16[5,4,128,128]{2,3,0,1:T(8,128)(2,1)S(1)}, u32[]{:S(2)}, u32[]{:S(2)}) collective-permute-start(bf16[5,4,128,128]{2,3,0,1:T(8,128)(2,1)S(1)} %convert_element_type.415), channel_id=1, source_target_pairs={{0,16},{16,0},{32,48},{48,32},{64,80},{80,64},{96,112},{112,96},{1... | collective-permute-start | bytes 1966088 | tf_op jit(solution)/shard_map/ppermute | solution.py:16
  173.3 19.1 %collective-permute-start.1 = (bf16[5,4,128,128]{2,3,0,1:T(8,128)(2,1)}, bf16[5,4,128,128]{2,3,0,1:T(8,128)(2,1)S(1)}, u32[]{:S(2)}, u32[]{:S(2)}) collective-permute-start(bf16[5,4,128,128]{2,3,0,1:T(8,128)(2,1)} %fusion.56), channel_id=1, source_target_pairs={{0,32},{16,48},{32,0},{48,16},{64,96},{80,112},{96,64},{112,80},{1... | collective-permute-start | bytes 1966088 | tf_op jit(solution)/shard_map/ppermute | solution.py:16
  193.6 110.6 %collective-permute-start.2 = (bf16[5,4,128,128]{2,3,0,1:T(8,128)(2,1)}, bf16[5,4,128,128]{2,3,0,1:T(8,128)(2,1)}, u32[]{:S(2)}, u32[]{:S(2)}) collective-permute-start(bf16[5,4,128,128]{2,3,0,1:T(8,128)(2,1)} %fusion.27), channel_id=1, source_target_pairs={{0,64},{16,80},{32,96},{48,112},{64,0},{80,16},{96,32},{112,48},{1... | collective-permute-start | bytes 1966088 | tf_op jit(solution)/shard_map/ppermute | solution.py:16
  301.4 7.6 %copy-start.6 = (f32[2,4,128,128]{3,2,1,0:T(8,128)S(1)}, f32[2,4,128,128]{3,2,1,0:T(8,128)}, u32[]{:S(2)}) copy-start(f32[2,4,128,128]{3,2,1,0:T(8,128)} %copy-done.5) | copy-start | bytes 1572868
  301.4 7.6 %copy-start.10 = (bf16[2,128,4,128]{3,2,1,0:T(4,128)(2,1)S(1)}, bf16[2,128,4,128]{3,2,1,0:T(4,128)(2,1)}, u32[]{:S(2)}) copy-start(bf16[2,128,4,128]{3,2,1,0:T(4,128)(2,1)} %copy-done.9) | copy-start | bytes 786436
  301.4 9.8 %collective-permute-start.5 = (f32[64,7,4]{0,2,1:T(4,128)S(1)}, f32[64,7,4]{0,2,1:T(4,128)S(1)}, u32[]{:S(2)}, u32[]{:S(2)}) collective-permute-start(f32[64,7,4]{0,2,1:T(4,128)S(1)} %convolution_bitcast_fusion.7), channel_id=1, source_target_pairs={{0,16},{16,0},{32,48},{48,32},{64,80},{80,64},{96,112},{112,96},{1... | collective-permute-start | bytes 21512 | tf_op jit(solution)/shard_map/ppermute | solution.py:158
  306.5 7.8 %copy-start.4 = (bf16[2,5,4,128,128]{3,4,1,2,0:T(8,128)(2,1)S(1)}, bf16[2,5,4,128,128]{3,4,1,2,0:T(8,128)(2,1)}, u32[]{:S(2)}) copy-start(bf16[2,5,4,128,128]{3,4,1,2,0:T(8,128)(2,1)} %copy-done.3) | copy-start | bytes 3932164
  306.5 7.8 %copy-start.16 = (bf16[2,1,4,128,128]{3,4,1,2,0:T(8,128)(2,1)S(1)}, bf16[2,1,4,128,128]{3,4,1,2,0:T(8,128)(2,1)}, u32[]{:S(2)}) copy-start(bf16[2,1,4,128,128]{3,4,1,2,0:T(8,128)(2,1)} %copy-done.15) | copy-start | bytes 786436
  306.5 32.7 %collective-permute-start.3 = (bf16[5,4,128,128]{2,3,0,1:T(8,128)(2,1)}, bf16[5,4,128,128]{2,3,0,1:T(8,128)(2,1)}, u32[]{:S(2)}, u32[]{:S(2)}) collective-permute-start(bf16[5,4,128,128]{2,3,0,1:T(8,128)(2,1)} %fusion.26), channel_id=1, source_target_pairs={{0,128},{16,144},{32,160},{48,176},{64,192},{80,208},{96,224},{112... | collective-permute-start | bytes 1966088 | tf_op jit(solution)/shard_map/ppermute | solution.py:16
  311.2 6.7 %collective-permute-start.6 = (f32[64,7,4]{0,2,1:T(4,128)S(1)}, f32[64,7,4]{0,2,1:T(4,128)S(1)}, u32[]{:S(2)}, u32[]{:S(2)}) collective-permute-start(f32[64,7,4]{0,2,1:T(4,128)S(1)} %add.360), channel_id=1, source_target_pairs={{0,32},{16,48},{32,0},{48,16},{64,96},{80,112},{96,64},{112,80},{1... | collective-permute-start | bytes 21512 | tf_op jit(solution)/shard_map/ppermute | solution.py:158
  318.0 29.2 %copy-start.12 = (f32[2,128,4,128]{3,1,2,0:T(8,128)S(1)}, f32[2,128,4,128]{3,1,2,0:T(8,128)}, u32[]{:S(2)}) copy-start(f32[2,128,4,128]{3,1,2,0:T(8,128)} %copy.219) | copy-start | bytes 1572868
  318.0 29.2 %copy-start.13 = (bf16[2,4,128,128]{3,2,1,0:T(8,128)(2,1)S(1)}, bf16[2,4,128,128]{3,2,1,0:T(8,128)(2,1)}, u32[]{:S(2)}) copy-start(bf16[2,4,128,128]{3,2,1,0:T(8,128)(2,1)} %fusion.11) | copy-start | bytes 786436
  318.0 29.4 %collective-permute-start.7 = (f32[64,7,4]{0,2,1:T(4,128)S(1)}, f32[64,7,4]{0,2,1:T(4,128)S(1)}, u32[]{:S(2)}, u32[]{:S(2)}) collective-permute-start(f32[64,7,4]{0,2,1:T(4,128)S(1)} %add.361), channel_id=1, source_target_pairs={{0,64},{16,80},{32,96},{48,112},{64,0},{80,16},{96,32},{112,48},{1... | collective-permute-start | bytes 21512 | tf_op jit(solution)/shard_map/ppermute | solution.py:158
  341.8 48.6 %collective-permute-start.4 = (bf16[5,4,128,128]{2,3,0,1:T(8,128)(2,1)}, bf16[5,4,128,128]{2,3,0,1:T(8,128)(2,1)}, u32[]{:S(2)}, u32[]{:S(2)}) collective-permute-start(bf16[5,4,128,128]{2,3,0,1:T(8,128)(2,1)} %add_convert_fusion), channel_id=1, source_target_pairs={{0,256},{16,272},{32,288},{48,304},{64,320},{80,336},{96,352},{112... | collective-permute-start | bytes 1966088 | tf_op jit(solution)/shard_map/ppermute | solution.py:16
  347.5 31.3 %collective-permute-start.8 = (f32[64,7,4]{0,2,1:T(4,128)S(1)}, f32[64,7,4]{0,2,1:T(4,128)S(1)}, u32[]{:S(2)}, u32[]{:S(2)}) collective-permute-start(f32[64,7,4]{0,2,1:T(4,128)S(1)} %add.362), channel_id=1, source_target_pairs={{0,128},{16,144},{32,160},{48,176},{64,192},{80,208},{96,224},{112... | collective-permute-start | bytes 21512 | tf_op jit(solution)/shard_map/ppermute | solution.py:158
  378.7 8.4 %collective-permute-start.9 = (f32[64,7,4]{0,2,1:T(4,128)S(1)}, f32[64,7,4]{0,2,1:T(4,128)S(1)}, u32[]{:S(2)}, u32[]{:S(2)}) collective-permute-start(f32[64,7,4]{0,2,1:T(4,128)S(1)} %add.363), channel_id=1, source_target_pairs={{0,256},{16,272},{32,288},{48,304},{64,320},{80,336},{96,352},{112... | collective-permute-start | bytes 21512 | tf_op jit(solution)/shard_map/ppermute | solution.py:158
  390.4 1.5 copy-start.11
  391.7 1.0 copy-start.14
  (1 other events, 0.7 us)
Sparse Core Ops, SparseCore 0:
  11.8 89.9 all-gather.2
